TPU v7x, 32 devices: a whole 2x2x4 slice. The times are simulated.
32 devices in a mesh: grp: 1, mid: 16 (over z, y, core), off: 2 (over x), sub: 1.
Axes of the slice: x: 2, y: 2, z: 4, core: 2. Of those that a mesh axis runs over, the one named last changes fastest.
Arguments:
- traces: bfloat16 [2, 1024, 1024], P('off', ('grp', 'mid'), 'sub'), may hold values from -6 to 6
- centre_offset: int32 [256], P(('grp', 'mid')), may hold values from 0 to 63
- foot_start: int32 [256, 16], P('grp'), may hold values from 0 to 240
- beam_count: int32 [16], P('grp'), may hold values from 2 to 16, as said below
- operator: bfloat16 [1024, 65536], P('sub', 'mid'), may hold values from -0.1875 to 0.1875
Outputs:
- image: float32 [256, 256], P(('grp', 'mid'))
Inputs may be any that keep to these rules, and one draw needn't show every extreme that they name: `beam_count`: the live beams of all tiles sum to exactly 128, and the largest count is exactly 16.
All inputs are finite; a program needn't handle non-finite values.
Results may differ from a plain program's by a relative error of at most 0.0028.
Values may be sent and summed in bfloat16 or wider, within the bound.
A program may use at most 64 MiB of HBM per device.

v0:
```python
import math

import jax
import jax.numpy as jnp
from jax import lax
from jax.sharding import PartitionSpec as P

NT = 1024
P_SIZE = 16
FL = 16
DEPTH = 256
HALF = 16
CB_DEV = 16


def padded_2(cells, sides, width):
    for axis, dim in sides:
        count = lax.axis_size(axis)
        ends = count - 1
        head = lax.slice_in_dim(cells, 0, width, axis=dim)
        tail = lax.slice_in_dim(cells, cells.shape[dim] - width, cells.shape[dim], axis=dim)
        cells = jnp.concatenate(
            [
                lax.ppermute(tail, axis, [(i, (i + 1) % count) for i in range(ends)]),
                cells,
                lax.ppermute(head, axis, [((i + 1) % count, i) for i in range(ends)]),
            ],
            axis=dim,
        )
    return cells


def dft_rows(first_row, row_count, freq_block):
    sample_index = first_row + jnp.arange(row_count, dtype=jnp.int32)[:, None]
    column = jnp.arange(NT, dtype=jnp.int32)[None, :]
    within = column % (2 * freq_block)
    frequency = column // (2 * freq_block) * freq_block + within % freq_block
    phase_angle = 2.0 * math.pi / NT * (sample_index * frequency % NT).astype(jnp.float32)
    values = jnp.where(within // freq_block == 1, -jnp.sin(phase_angle), jnp.cos(phase_angle))
    return values / math.sqrt(NT)


def slant_weights(frequency):
    offsets = jnp.arange(-HALF, HALF + 1, dtype=jnp.int32).astype(jnp.float32)
    taper = jnp.exp(-0.5 * (1.5 * offsets / HALF) ** 2)
    taper = taper / jnp.sqrt(jnp.sum(taper * taper))
    slopes = 0.25 * (jnp.arange(P_SIZE, dtype=jnp.int32).astype(jnp.float32) - 0.5 * (P_SIZE - 1))
    theta = (
        2.0
        * math.pi
        / NT
        * slopes[:, None, None]
        * offsets[None, :, None]
        * frequency.astype(jnp.float32)[None, None, :]
    )
    return (taper[None, :, None] * jnp.cos(theta), taper[None, :, None] * jnp.sin(theta))


def form_beams(windows_real, windows_imag, cos_weight, sin_weight):
    high = lax.Precision.HIGHEST
    beam_real = jnp.einsum("pxf,bxf->bpf", cos_weight, windows_real, precision=high) + jnp.einsum(
        "pxf,bxf->bpf", sin_weight, windows_imag, precision=high
    )
    beam_imag = jnp.einsum("pxf,bxf->bpf", cos_weight, windows_imag, precision=high) - jnp.einsum(
        "pxf,bxf->bpf", sin_weight, windows_real, precision=high
    )
    return (beam_real, beam_imag)


def live_rows(beam_count, per_tile, live_total):
    tile_ends = jnp.cumsum(beam_count)
    position = jnp.arange(live_total, dtype=jnp.int32)
    owner = jnp.sum((position[:, None] >= tile_ends[None, :]).astype(jnp.int32), axis=1)
    first = tile_ends - beam_count
    match = owner[:, None] == jnp.arange(beam_count.shape[0], dtype=jnp.int32)[None, :]
    chosen = jnp.sum(jnp.where(match, first[None, :], 0), axis=1)
    return owner * per_tile + position - chosen


def spread_slopes(beams, mid_count):
    return jnp.repeat(beams, mid_count // P_SIZE, axis=1)[:, :, None, :]


def shards(traces, centre_offset, foot_start, beam_count, operator):
    high = lax.Precision.HIGHEST
    mid_count = lax.axis_size("mid")
    mid_index = lax.axis_index("mid")
    sub_index = lax.axis_index("sub")
    samples = traces.shape[2]
    freq_block = samples // 2
    dft_table = dft_rows(sub_index * samples, samples, freq_block)
    partial_value = jnp.dot(traces[0].astype(jnp.float32), dft_table, precision=high)
    spectrum = lax.psum_scatter(partial_value, "sub", scatter_dimension=1, tiled=True)
    padded = padded_2(spectrum, (("mid", 0),), HALF)
    window_index = centre_offset[:, None] + jnp.arange(2 * HALF + 1, dtype=jnp.int32)[None, :]
    windows = padded[window_index]
    frequency = sub_index * freq_block + jnp.arange(freq_block, dtype=jnp.int32)
    cos_weight, sin_weight = slant_weights(frequency)
    beam_real, beam_imag = form_beams(
        windows[:, :, :freq_block], windows[:, :, freq_block:], cos_weight, sin_weight
    )
    live_here = lax.dynamic_index_in_dim(beam_count, mid_index, 0, keepdims=False)
    alive = jnp.arange(CB_DEV, dtype=jnp.int32) < live_here
    beams = jnp.where(
        alive[:, None, None], jnp.concatenate([beam_real, beam_imag], axis=2), 0.0
    ).astype(jnp.bfloat16)
    columns = operator.shape[1]
    slope_count = max(1, P_SIZE // mid_count)
    footprint_size = FL * DEPTH
    first_column = mid_index * columns
    slope_first = first_column // footprint_size
    lateral_first = first_column % footprint_size // DEPTH
    lateral_count = columns // (slope_count * DEPTH)
    starts = lax.dynamic_slice_in_dim(foot_start, slope_first, slope_count, 1)
    kernels = operator.reshape(samples, slope_count, lateral_count * DEPTH)
    outgoing = spread_slopes(beams, mid_count)
    received = lax.all_to_all(outgoing, "mid", split_axis=1, concat_axis=0, tiled=True)
    row_total = received.shape[0]
    received = received.reshape(row_total, slope_count, samples)
    chosen = live_rows(beam_count, CB_DEV, row_total // 2)
    received = received[chosen]
    starts = starts[chosen]
    centres_all = CB_DEV * mid_count
    block_rows = received.shape[0] // 8
    lateral_steps = lateral_first + jnp.arange(lateral_count, dtype=jnp.int32)
    weight_scale = 1.0 / math.sqrt(FL * P_SIZE)

    def add_block(block, partial_image):
        block_beams = lax.dynamic_slice_in_dim(received, block * block_rows, block_rows, 0)
        block_starts = lax.dynamic_slice_in_dim(starts, block * block_rows, block_rows, 0)
        footprint = (
            jnp.einsum(
                "rsk,ksc->rsc",
                block_beams,
                kernels,
                preferred_element_type=jnp.float32,
                precision=None,
            )
            * weight_scale
        )
        target = (block_starts[:, :, None] + lateral_steps[None, None, :]).reshape(-1)
        return partial_image.at[target].add(footprint.reshape(-1, DEPTH))

    partial_image = lax.fori_loop(0, 8, add_block, jnp.zeros((centres_all, DEPTH), jnp.float32))
    tile_part = lax.psum_scatter(partial_image, "mid", scatter_dimension=0, tiled=True)
    image_tile = lax.psum(tile_part, ("off", "sub"))
    return image_tile


def solution(mesh):
    return jax.shard_map(
        shards,
        mesh=mesh,
        in_specs=(
            P("off", ("grp", "mid"), "sub"),
            P(("grp", "mid")),
            P("grp", None),
            P("grp"),
            P("sub", "mid"),
        ),
        out_specs=P(("grp", "mid"), None),
        check_vma=False,
    )
```

profile of v0, /device:TPU:0, one launch (start us, length us, event | category | flops | bytes accessed | tf_op | source)
XLA Modules:
  0.0 302.9 jit_solution(10258780660640773657)
XLA Ops:
  7.4 19.2 %fusion.60 = f32[64,1024]{1,0:T(8,128)S(1)} fusion(s32[1024]{0:T(1024)S(1)} %fusion.67, pred[1024]{0:T(1024)(128)(4,1)S(1)} %fusion.64, bf16[1,64,1024]{2,1,0:T(8,128)(2,1)S(1)} %copy-done), kind=kOutput, calls=%fused_computation.61 | convolution fusion | flops 823132160 | bytes 398336 | tf_op jit(solution)/shard_map/dot_general | solution.py:92
  26.7 2.4 collective-permute-start
  34.4 2.5 gather_fusion.1
  40.5 3.7 %copy.23 = f32[16,33,512]{1,0,2:T(8,128)} copy(f32[16,33,512]{2,1,0:T(8,128)S(1)} %get-tuple-element.148) | data formatting | bytes 2162688
  44.2 3.8 %copy.24 = f32[16,33,512]{1,0,2:T(8,128)} copy(f32[16,33,512]{2,1,0:T(8,128)S(1)} %get-tuple-element.149) | data formatting | bytes 2162688
  48.0 24.9 %fusion.16 = f32[512,16,16]{2,1,0:T(8,128)S(1)} fusion(f32[16,33,512]{1,0,2:T(8,128)} %copy.23, f32[512]{0:T(512)S(1)} %iota_convert_fusion, f32[16,33]{1,0:T(8,128)S(1)} %broadcast_multiply_fusion, f32[33]{0:T(128)S(1)} %broadcast_divide_fusion), kind=kOutput, calls=%fused_computation.24 | convolution fusion | flops 52445184 | bytes 1609924 | tf_op jit(solution)/shard_map/pxf,bxf->bpf/dot_general | solution.py:61
  72.9 22.2 %fusion.14 = f32[512,16,16]{2,1,0:T(8,128)S(1)} fusion(f32[16,33,512]{1,0,2:T(8,128)S(1)} %copy-done.3, f32[512]{0:T(512)S(1)} %iota_convert_fusion, f32[16,33]{1,0:T(8,128)S(1)} %broadcast_multiply_fusion, f32[33]{0:T(128)S(1)} %broadcast_divide_fusion), kind=kOutput, calls=%fused_computation.23 | convolution fusion | flops 52445184 | bytes 1609924 | tf_op jit(solution)/shard_map/pxf,bxf->bpf/dot_general | solution.py:64
  95.1 23.7 %add_bitcast_fusion = bf16[16,16,1,512]{1,0,3,2:T(8,128)(2,1)S(1)} fusion(f32[512,16,16]{2,1,0:T(8,128)S(1)} %fusion.16, f32[16,33,512]{1,0,2:T(8,128)S(1)} %copy-done.3, f32[512]{0:T(512)S(1)} %iota_convert_fusion, f32[16,33]{1,0:T(8,128)S(1)} %broadcast_multiply_fusion, f32[33]{0:T(128)S(1)} %broadcast_divide_fusion), kind=kOutput, calls=%fused_computation.32 | convolution fusion | flops 52707328 | bytes 1872068 | tf_op jit(solution)/shard_map/pxf,bxf->bpf/dot_general | solution.py:61
  118.9 23.7 %subtract_bitcast_fusion = bf16[16,16,1,512]{1,0,3,2:T(8,128)(2,1)S(1)} fusion(f32[512,16,16]{2,1,0:T(8,128)S(1)} %fusion.14, f32[16,33,512]{1,0,2:T(8,128)S(1)} %copy-done.2, f32[512]{0:T(512)S(1)} %iota_convert_fusion, f32[16,33]{1,0:T(8,128)S(1)} %broadcast_multiply_fusion, f32[33]{0:T(128)S(1)} %broadcast_divide_fusion), kind=kOutput, calls=%fused_computation.31 | convolution fusion | flops 52707328 | bytes 1872068 | tf_op jit(solution)/shard_map/pxf,bxf->bpf/dot_general | solution.py:64
  142.6 2.6 maximum_select_fusion
  145.2 5.7 %copy.22 = bf16[16,16,1,1024]{3,0,2,1:T(8,128)(2,1)} copy(bf16[16,16,1,1024]{1,0,3,2:T(8,128)(2,1)} %maximum_select_fusion) | data formatting | bytes 1048576 | tf_op jit(solution)/shard_map/jit(_where)/select_n | solution.py:104
  150.8 8.4 %all-to-all-start = ((bf16[16,16,1,1024]{3,0,2,1:T(8,128)(2,1)}), bf16[16,16,1,1024]{3,0,2,1:T(8,128)(2,1)S(1)}, u32[]{:S(2)}, u32[]{:S(2)}) async-start(bf16[16,16,1,1024]{3,0,2,1:T(8,128)(2,1)} %copy.22), calls=%async_computation | async-start | bytes 1048576 | tf_op jit(solution)/shard_map/all_to_all | solution.py:117
  162.0 11.5 %all-to-all-done = bf16[16,16,1,1024]{3,0,2,1:T(8,128)(2,1)S(1)} async-done(((bf16[16,16,1,1024]{3,0,2,1:T(8,128)(2,1)}), bf16[16,16,1,1024]{3,0,2,1:T(8,128)(2,1)S(1)}, u32[]{:S(2)}, u32[]{:S(2)}) %all-to-all-start) | async-done | bytes 524320 | tf_op jit(solution)/shard_map/all_to_all | solution.py:117
  174.4 56.2 %while.14 = (s32[]{:T(128)}, f32[256,256]{1,0:T(8,128)S(1)}, s32[128,1]{0,1:T(1,128)S(1)}, bf16[128,1,1024]{2,0,1:T(8,128)(2,1)S(1)}, bf16[1024,1,4096]{2,0,1:T(...) while((s32[]{:T(128)}, f32[256,256]{1,0:T(8,128)S(1)}, ...), condition=%wide.region_6.7_spmd.clone, body=%wide.region_4.6_spmd.clone.sunk | while | flops 134349840 | bytes 10000863 | solution.py:144
  174.4 4.6 %fusion.92 = f32[16,1,4096]{2,0,1:T(8,128)S(1)} fusion(bf16[1024,1,4096]{2,0,1:T(8,128)(2,1)} %get-tuple-element.213, bf16[128,1,1024]{2,0,1:T(8,128)(2,1)S(1)} %get-tuple-element.212, s32[]{:T(128)S(6)} %select_n.211), kind=kOutput, calls=%fused_computation.8.clone.1 | convolution fusion | flops 134283264 | bytes 8683524 | tf_op jit(solution)/shard_map/while/body/eval_jaxpr/rsk,ksc->rsc/dot_general | solution.py:132
  181.4 4.6 %fusion.92 = f32[16,1,4096]{2,0,1:T(8,128)S(1)} fusion(bf16[1024,1,4096]{2,0,1:T(8,128)(2,1)} %get-tuple-element.213, bf16[128,1,1024]{2,0,1:T(8,128)(2,1)S(1)} %get-tuple-element.212, s32[]{:T(128)S(6)} %select_n.211), kind=kOutput, calls=%fused_computation.8.clone.1 | convolution fusion | flops 134283264 | bytes 8683524 | tf_op jit(solution)/shard_map/while/body/eval_jaxpr/rsk,ksc->rsc/dot_general | solution.py:132
  188.4 4.6 %fusion.92 = f32[16,1,4096]{2,0,1:T(8,128)S(1)} fusion(bf16[1024,1,4096]{2,0,1:T(8,128)(2,1)} %get-tuple-element.213, bf16[128,1,1024]{2,0,1:T(8,128)(2,1)S(1)} %get-tuple-element.212, s32[]{:T(128)S(6)} %select_n.211), kind=kOutput, calls=%fused_computation.8.clone.1 | convolution fusion | flops 134283264 | bytes 8683524 | tf_op jit(solution)/shard_map/while/body/eval_jaxpr/rsk,ksc->rsc/dot_general | solution.py:132
  195.5 4.6 %fusion.92 = f32[16,1,4096]{2,0,1:T(8,128)S(1)} fusion(bf16[1024,1,4096]{2,0,1:T(8,128)(2,1)} %get-tuple-element.213, bf16[128,1,1024]{2,0,1:T(8,128)(2,1)S(1)} %get-tuple-element.212, s32[]{:T(128)S(6)} %select_n.211), kind=kOutput, calls=%fused_computation.8.clone.1 | convolution fusion | flops 134283264 | bytes 8683524 | tf_op jit(solution)/shard_map/while/body/eval_jaxpr/rsk,ksc->rsc/dot_general | solution.py:132
  202.5 4.6 %fusion.92 = f32[16,1,4096]{2,0,1:T(8,128)S(1)} fusion(bf16[1024,1,4096]{2,0,1:T(8,128)(2,1)} %get-tuple-element.213, bf16[128,1,1024]{2,0,1:T(8,128)(2,1)S(1)} %get-tuple-element.212, s32[]{:T(128)S(6)} %select_n.211), kind=kOutput, calls=%fused_computation.8.clone.1 | convolution fusion | flops 134283264 | bytes 8683524 | tf_op jit(solution)/shard_map/while/body/eval_jaxpr/rsk,ksc->rsc/dot_general | solution.py:132
  209.5 4.6 %fusion.92 = f32[16,1,4096]{2,0,1:T(8,128)S(1)} fusion(bf16[1024,1,4096]{2,0,1:T(8,128)(2,1)} %get-tuple-element.213, bf16[128,1,1024]{2,0,1:T(8,128)(2,1)S(1)} %get-tuple-element.212, s32[]{:T(128)S(6)} %select_n.211), kind=kOutput, calls=%fused_computation.8.clone.1 | convolution fusion | flops 134283264 | bytes 8683524 | tf_op jit(solution)/shard_map/while/body/eval_jaxpr/rsk,ksc->rsc/dot_general | solution.py:132
  216.5 4.6 %fusion.92 = f32[16,1,4096]{2,0,1:T(8,128)S(1)} fusion(bf16[1024,1,4096]{2,0,1:T(8,128)(2,1)} %get-tuple-element.213, bf16[128,1,1024]{2,0,1:T(8,128)(2,1)S(1)} %get-tuple-element.212, s32[]{:T(128)S(6)} %select_n.211), kind=kOutput, calls=%fused_computation.8.clone.1 | convolution fusion | flops 134283264 | bytes 8683524 | tf_op jit(solution)/shard_map/while/body/eval_jaxpr/rsk,ksc->rsc/dot_general | solution.py:132
  223.5 4.6 %fusion.92 = f32[16,1,4096]{2,0,1:T(8,128)S(1)} fusion(bf16[1024,1,4096]{2,0,1:T(8,128)(2,1)} %get-tuple-element.213, bf16[128,1,1024]{2,0,1:T(8,128)(2,1)S(1)} %get-tuple-element.212, s32[]{:T(128)S(6)} %select_n.211), kind=kOutput, calls=%fused_computation.8.clone.1 | convolution fusion | flops 134283264 | bytes 8683524 | tf_op jit(solution)/shard_map/while/body/eval_jaxpr/rsk,ksc->rsc/dot_general | solution.py:132
  231.3 55.4 %reduce-scatter.2.cloned.1.call-done = f32[16,256]{1,0:T(8,128)} async-done(((f32[256,256]{1,0:T(8,128)}), f32[16,256]{1,0:T(8,128)}) %reduce-scatter.2.cloned.1.call-update) | async-done | bytes 16400 | tf_op jit(solution)/shard_map/reduce_scatter | solution.py:145
  286.7 9.4 %psum.7 = f32[16,256]{1,0:T(8,128)} all-reduce(f32[16,256]{1,0:T(8,128)} %reduce-scatter.2.cloned.1.call-done), channel_id=1, replica_groups=mesh['grp'=1,'mid'=16,'off'=2,'sub'=1] {'off','sub'}, use_global_device_ids=true, to_apply=%region_8.9 | all-reduce | flops 4096 | bytes 32768 | tf_op jit(solution)/shard_map/psum | solution.py:146
  (102 shorter events, 32.4 us)
Async XLA Ops:
  6.5 0.9 copy-start
  7.4 23.8 %copy-start.4 = (s32[16]{0:T(128)S(1)}, s32[16]{0:T(128)}, u32[]{:S(2)}) copy-start(s32[16]{0:T(128)} %param.8) | copy-start | bytes 196
  7.4 24.7 %copy-start.5 = (s32[16]{0:T(128)S(1)}, s32[16]{0:T(128)}, u32[]{:S(2)}) copy-start(s32[16]{0:T(128)} %param.10) | copy-start | bytes 196
  26.7 6.7 %collective-permute-start = (f32[16,1024]{1,0:T(8,128)S(1)}, f32[16,1024]{1,0:T(8,128)S(1)}, u32[]{:S(2)}, u32[]{:S(2)}) collective-permute-start(f32[16,1024]{1,0:T(8,128)S(1)} %get-tuple-element.150), channel_id=1, source_target_pairs={{0,2},{2,4},{4,6},{6,8},{8,10},{10,12},{12,14},{14,16},{16,18},{18... | collective-permute-start | bytes 196616 | tf_op jit(solution)/shard_map/ppermute | solution.py:24
  29.1 5.3 %collective-permute-start.1 = (f32[16,1024]{1,0:T(8,128)S(1)}, f32[16,1024]{1,0:T(8,128)S(1)}, u32[]{:S(2)}, u32[]{:S(2)}) collective-permute-start(f32[16,1024]{1,0:T(8,128)S(1)} %get-tuple-element.151), channel_id=1, source_target_pairs={{2,0},{4,2},{6,4},{8,6},{10,8},{12,10},{14,12},{16,14},{18,16},{20... | collective-permute-start | bytes 196616 | tf_op jit(solution)/shard_map/ppermute | solution.py:26
  48.0 24.9 %copy-start.3 = (f32[16,33,512]{1,0,2:T(8,128)S(1)}, f32[16,33,512]{1,0,2:T(8,128)}, u32[]{:S(2)}) copy-start(f32[16,33,512]{1,0,2:T(8,128)} %copy.24) | copy-start | bytes 3244036
  95.1 23.8 %copy-start.2 = (f32[16,33,512]{1,0,2:T(8,128)S(1)}, f32[16,33,512]{1,0,2:T(8,128)}, u32[]{:S(2)}) copy-start(f32[16,33,512]{1,0,2:T(8,128)} %copy.23) | copy-start | bytes 3244036
  150.8 22.7 %all-to-all-start = ((bf16[16,16,1,1024]{3,0,2,1:T(8,128)(2,1)}), bf16[16,16,1,1024]{3,0,2,1:T(8,128)(2,1)S(1)}, u32[]{:S(2)}, u32[]{:S(2)}) async-start(bf16[16,16,1,1024]{3,0,2,1:T(8,128)(2,1)} %copy.22), calls=%async_computation | async-start | bytes 1048576 | tf_op jit(solution)/shard_map/all_to_all | solution.py:117
  159.2 127.5 %reduce-scatter.2.cloned.1.call-start = ((), (), s32[]{:S(2)}) async-start(), calls=%async_computation.2 | async-start | bytes 278528 | tf_op jit(solution)/shard_map/reduce_scatter | solution.py:145
  230.5 0.7 copy-start.1
Sparse Core Ops, SparseCore 0:
  231.4 55.2 reduce-scatter.1
where the time goes:
time: 304 us; the launch traced here: 303 us
  matrix products  150 us (49%)
  waiting for transfers between devices  67.9 us (22%)
  local copies, waits for them, and re-layouts  26.1 us (9%)
  other arithmetic  21.8 us (7%)
  between operations  14.4 us (5%)
  starting transfers between devices  12.5 us (4%)
  blocking collectives  9.37 us (3%)
    reduce_scatter x1, waiting for transfers between devices, shards(): lax.psum_scatter(partial_image, 'mid', scatter_dimension=0, tiled=True)  55.4 us
    dot_general x8, matrix products, add_block(): jnp.einsum('rsk,ksc->rsc', block_beams, kernels, preferred_element_type=j...  36.7 us
    dot_general x1, matrix products, form_beams(): jnp.einsum('pxf,bxf->bpf', cos_weight, windows_real, precision=high)  24.9 us
    dot_general x1, matrix products, form_beams(): jnp.einsum('pxf,bxf->bpf', sin_weight, windows_imag, precision=high)  23.7 us
    dot_general x1, matrix products, form_beams(): jnp.einsum('pxf,bxf->bpf', sin_weight, windows_real, precision=high)  23.7 us
    dot_general x1, matrix products, form_beams(): jnp.einsum('pxf,bxf->bpf', cos_weight, windows_imag, precision=high)  22.2 us
    dot_general x1, matrix products, shards(): jnp.dot(traces[0].astype(jnp.float32), dft_table, precision=high)  19.2 us
    scatter-add x8, other arithmetic, add_block(): return partial_image.at[target].add(footprint.reshape(-1, DEPTH))  16.6 us
  transfers between devices with their start and end apart: 4, of which 3 were waited for; matrix products, arithmetic and copies ran while one was open for 1% of the time, Pallas kernels for 0%

commit v1 on v0

v1 whole, which is shorter than its diff:
```python
import functools
import math

import jax
import jax.numpy as jnp
import numpy as np
from jax import lax
from jax.experimental import pallas as pl
from jax.experimental.pallas import tpu as pltpu
from jax.sharding import PartitionSpec as P

P_SIZE = 16
FL = 16
DEPTH = 256
HALF = 16
LANES = 128
F32 = jnp.float32
BF16 = jnp.bfloat16


def dft_quarter(total, parts):
    block = total // 2 // parts
    frequency = np.arange(total // 2)
    phase = 2.0 * np.pi / total * (np.arange(total // 4)[:, None] * frequency[None, :] % total)
    pair = np.stack([np.cos(phase), -np.sin(phase)]) / math.sqrt(total)
    pair = pair.reshape(2, total // 4, parts, block // LANES, LANES)
    table = pair.transpose(2, 1, 3, 0, 4).reshape(parts, total // 4, 2 * block).astype(np.float32)
    high = table.astype(BF16)
    low = (table - high.astype(np.float32)).astype(BF16)
    return high, low


def half_weights(total, parts):
    offsets = np.arange(-HALF, HALF + 1)
    taper = np.exp(-0.5 * (1.5 * offsets / HALF) ** 2)
    taper = (taper / np.sqrt(np.sum(taper * taper)))[HALF:]
    slopes = 0.25 * (np.arange(P_SIZE // 2, P_SIZE) - 0.5 * (P_SIZE - 1))
    theta = (
        2.0 * np.pi / total
        * np.arange(HALF + 1)[:, None, None] * slopes[None, :, None]
        * np.arange(total // 2)[None, None, :]
    )
    both = np.stack([np.cos(theta), np.sin(theta)]) * taper[None, :, None, None]
    both = both.reshape(2, HALF + 1, P_SIZE // 2, parts, -1).transpose(3, 0, 1, 2, 4)
    return both.astype(np.float32)


def kernel(
    sizes,
    traces_ref, offset_ref, start_ref, count_ref, operator_ref, high_ref, low_ref, weight_ref,
    out_ref,
    ext, high, low, weight, oper, spec, stage, send, recv, gathered, image, parts, tile, peers,
    load_sem, halo_send, halo_recv, beam_send, beam_recv, part_send, part_recv, peer_send, peer_recv,
):
    mids, offs, subs = sizes
    rep = mids // P_SIZE
    me = lax.axis_index("mid")
    group = offs * subs
    mine = lax.axis_index("off") * subs + lax.axis_index("sub")
    rows = traces_ref.shape[0]
    total = traces_ref.shape[1]
    quarter = total // 4
    samples = operator_ref.shape[0]
    block = samples // 2
    chunks = block // LANES
    beams = offset_ref.shape[0]
    laterals = operator_ref.shape[1] // DEPTH
    first_freq = lax.axis_index("sub") * block

    def member(k):
        other = lax.rem(mine + k, group)
        return other, {"off": other // subs, "sub": lax.rem(other, subs)}

    load_ext = pltpu.make_async_copy(traces_ref, ext.at[pl.ds(HALF, rows)], load_sem.at[0])
    load_high = pltpu.make_async_copy(high_ref, high, load_sem.at[1])
    load_low = pltpu.make_async_copy(low_ref, low, load_sem.at[2])
    load_weight = pltpu.make_async_copy(weight_ref, weight, load_sem.at[3])
    load_oper = pltpu.make_async_copy(operator_ref, oper, load_sem.at[4])
    load_ext.start()
    load_high.start()
    load_low.start()
    load_weight.start()
    load_oper.start()

    barrier = pltpu.get_barrier_semaphore()

    @pl.loop(1, mids)
    def _(k):
        pl.semaphore_signal(barrier, inc=1, device_id={"mid": lax.rem(me + k, mids)})

    @pl.loop(1, group)
    def _(k):
        pl.semaphore_signal(barrier, inc=1, device_id=member(k)[1])

    pl.semaphore_wait(barrier, mids - 1 + group - 1)

    right, left = lax.rem(me + 1, mids), lax.rem(me + mids - 1, mids)
    to_right = pltpu.make_async_remote_copy(
        traces_ref.at[pl.ds(rows - HALF, HALF)], ext.at[pl.ds(0, HALF)],
        halo_send.at[0], halo_recv.at[0], device_id={"mid": right},
    )
    to_left = pltpu.make_async_remote_copy(
        traces_ref.at[pl.ds(0, HALF)], ext.at[pl.ds(HALF + rows, HALF)],
        halo_send.at[1], halo_recv.at[1], device_id={"mid": left},
    )
    to_right.start()
    to_left.start()

    centres = start_ref.shape[0]
    slope = me // rep
    lateral_first = lax.rem(me, rep) * laterals
    lane = lax.broadcasted_iota(jnp.int32, start_ref.shape, 1)
    starts = jnp.sum(jnp.where(lane == slope, start_ref[...], 0), axis=1, keepdims=True)
    beam_id = lax.broadcasted_iota(jnp.int32, (centres, mids), 0)
    tile_id = lax.broadcasted_iota(jnp.int32, (centres, mids), 1)
    slot = beam_id - tile_id * beams
    alive = (slot >= 0) & (slot < count_ref[...])
    alive = jnp.sum(jnp.where(alive, 1, 0), axis=1, keepdims=True)
    target = jnp.where(alive > 0, starts + lateral_first, -1)
    hot = (target == lax.broadcasted_iota(jnp.int32, (centres, centres), 1)).astype(F32)
    hot = hot.T.astype(BF16)

    load_ext.wait()
    load_high.wait()
    load_low.wait()
    to_right.wait()
    to_left.wait()

    inside_low = (me > 0).astype(F32)
    inside_high = (me < mids - 1).astype(F32)
    row = lax.broadcasted_iota(jnp.int32, (rows + 2 * HALF, LANES), 0)
    keep = jnp.where(row < HALF, inside_low, jnp.where(row >= HALF + rows, inside_high, 1.0))
    stacked = jnp.concatenate([ext[:, q * quarter:(q + 1) * quarter] for q in range(4)], axis=0)
    count = rows + 2 * HALF
    for c in range(chunks):
        wide = slice(2 * c * LANES, 2 * (c + 1) * LANES)
        y = jnp.dot(stacked, high[:, wide], preferred_element_type=F32)
        y = y + jnp.dot(stacked, low[:, wide], preferred_element_type=F32)
        y0, y1, y2, y3 = (y[q * count:(q + 1) * count] for q in range(4))
        even_sum, even_dif, odd_sum, odd_dif = y0 + y2, y0 - y2, y1 + y3, y1 - y3
        f = first_freq + c * LANES + lax.broadcasted_iota(jnp.int32, (count, LANES), 1)
        phase = lax.rem(f, 4)
        sign = jnp.where(phase < 2, 1.0, -1.0)
        odd = lax.rem(f, 2) == 1
        real = jnp.where(
            odd, even_dif[:, :LANES] + sign * odd_dif[:, LANES:],
            even_sum[:, :LANES] + sign * odd_sum[:, :LANES],
        ) * keep
        imag = jnp.where(
            odd, even_dif[:, LANES:] - sign * odd_dif[:, :LANES],
            even_sum[:, LANES:] + sign * odd_sum[:, LANES:],
        ) * keep
        pairs = P_SIZE // 2
        spec[:, :, c * LANES:(c + 1) * LANES] = jnp.broadcast_to(
            real[:, None, :], (count, pairs, LANES))
        spec[:, :, block + c * LANES:block + (c + 1) * LANES] = jnp.broadcast_to(
            imag[:, None, :], (count, pairs, LANES))

    load_weight.wait()
    pairs = P_SIZE // 2

    @pl.loop(0, beams)
    def _(b):
        centre = offset_ref[b] + HALF
        for c in range(chunks):
            re = slice(c * LANES, (c + 1) * LANES)
            im = slice(block + c * LANES, block + (c + 1) * LANES)
            cos0 = weight[0, 0, :, re]
            a_re = cos0 * spec[centre, :, re]
            a_im = cos0 * spec[centre, :, im]
            b_re = jnp.zeros_like(a_re)
            b_im = jnp.zeros_like(a_re)
            for x in range(1, HALF + 1):
                r_up, r_dn = spec[centre + x, :, re], spec[centre - x, :, re]
                i_up, i_dn = spec[centre + x, :, im], spec[centre - x, :, im]
                cos, sin = weight[0, x, :, re], weight[1, x, :, re]
                a_re += cos * (r_up + r_dn)
                a_im += cos * (i_up + i_dn)
                b_re += sin * (i_up - i_dn)
                b_im += sin * (r_up - r_dn)
            at = pl.ds(pl.multiple_of(b * pairs, pairs), pairs)
            stage[c, 0, at, :] = a_re + b_re
            stage[c, 1, at, :] = a_im - b_im
            stage[c, 2, at, :] = a_re - b_re
            stage[c, 3, at, :] = a_im + b_im

    for p in range(pairs):
        for c in range(chunks):
            for part in range(2):
                lanes = slice(part * block + c * LANES, part * block + (c + 1) * LANES)
                every = pl.ds(p, beams, stride=pairs)
                send[pairs + p, :, lanes] = stage.at[c, part][every, :].astype(BF16)
                send[pairs - 1 - p, :, lanes] = stage.at[c, 2 + part][every, :].astype(BF16)

    def beam_copy(k, to, source):
        return pltpu.make_async_remote_copy(
            send.at[to // rep], recv.at[pl.ds(pl.multiple_of(source * beams, beams), beams)],
            beam_send.at[k], beam_recv.at[source], device_id={"mid": to},
        )

    @pl.loop(1, mids)
    def _(k):
        beam_copy(k, lax.rem(me + k, mids), me).start()

    recv[pl.ds(pl.multiple_of(me * beams, beams), beams), :] = send[slope]

    @pl.loop(1, mids)
    def _(k):
        beam_copy(k, lax.rem(me + k, mids), lax.rem(me + mids - k, mids)).wait()

    gathered[...] = jnp.dot(hot, recv[...], preferred_element_type=F32).astype(BF16)
    load_oper.wait()
    image[...] = jnp.zeros_like(image)

    @pl.loop(0, laterals)
    def _(step):
        l = laterals - 1 - step
        columns = pl.ds(pl.multiple_of(l * DEPTH, DEPTH), DEPTH)
        foot = jnp.dot(gathered[...], oper[:, columns], preferred_element_type=F32)
        image[...] = pltpu.roll(image[...], 1, 0) + foot

    def part_copy(k, to, source):
        return pltpu.make_async_remote_copy(
            image.at[pl.ds(pl.multiple_of(to * beams, beams), beams)], parts.at[source],
            part_send.at[k], part_recv.at[source], device_id={"mid": to},
        )

    @pl.loop(1, mids)
    def _(k):
        part_copy(k, lax.rem(me + k, mids), me).start()

    parts[me] = image[pl.ds(pl.multiple_of(me * beams, beams), beams), :]

    @pl.loop(1, mids)
    def _(k):
        part_copy(k, lax.rem(me + k, mids), lax.rem(me + mids - k, mids)).wait()

    tile[...] = jnp.sum(parts[...], axis=0) * (1.0 / math.sqrt(FL * P_SIZE))

    def peer_copy(k, to, source):
        return pltpu.make_async_remote_copy(
            tile, peers.at[source], peer_send.at[k], peer_recv.at[source], device_id=to,
        )

    @pl.loop(1, group)
    def _(k):
        peer_copy(k, member(k)[1], mine).start()

    peers[mine] = tile[...]

    @pl.loop(1, group)
    def _(k):
        peer_copy(k, member(k)[1], lax.rem(mine + group - k, group)).wait()

    out_ref[...] = jnp.sum(peers[...], axis=0)


def shards(traces, centre_offset, foot_start, beam_count, operator):
    mids, offs, subs = (lax.axis_size(name) for name in ("mid", "off", "sub"))
    traces = traces[0]
    if subs > 1:
        traces = lax.all_gather(traces, "sub", axis=1, tiled=True)
    rows, total = traces.shape
    samples, columns = operator.shape
    beams = centre_offset.shape[0]
    centres = foot_start.shape[0]
    group = offs * subs
    high, low = dft_quarter(total, subs)
    weight = half_weights(total, subs)
    pick = (lambda table: table[0]) if subs == 1 else (
        lambda table: lax.dynamic_index_in_dim(jnp.asarray(table), lax.axis_index("sub"), 0, False))
    high, low, weight = (jnp.asarray(pick(table)) for table in (high, low, weight))
    vmem = pl.BlockSpec(memory_space=pltpu.VMEM)
    smem = pl.BlockSpec(memory_space=pltpu.SMEM)
    hbm = pl.BlockSpec(memory_space=pl.ANY)
    dma = pltpu.SemaphoreType.DMA
    chunks = samples // 2 // LANES
    return pl.pallas_call(
        functools.partial(kernel, (mids, offs, subs)),
        out_shape=jax.ShapeDtypeStruct((beams, DEPTH), F32),
        in_specs=[hbm, smem, vmem, vmem, hbm, hbm, hbm, hbm],
        out_specs=vmem,
        scratch_shapes=[
            pltpu.VMEM((rows + 2 * HALF, total), BF16),
            pltpu.VMEM(high.shape, BF16),
            pltpu.VMEM(low.shape, BF16),
            pltpu.VMEM(weight.shape, F32),
            pltpu.VMEM((samples, columns), BF16),
            pltpu.VMEM((rows + 2 * HALF, P_SIZE // 2, samples), F32),
            pltpu.VMEM((chunks, 4, beams * P_SIZE // 2, LANES), F32),
            pltpu.VMEM((P_SIZE, beams, samples), BF16),
            pltpu.VMEM((mids * beams, samples), BF16),
            pltpu.VMEM((centres, samples), BF16),
            pltpu.VMEM((centres, DEPTH), F32),
            pltpu.VMEM((mids, beams, DEPTH), F32),
            pltpu.VMEM((beams, DEPTH), F32),
            pltpu.VMEM((group, beams, DEPTH), F32),
            dma((5,)),
            dma((2,)),
            dma((2,)),
            dma((mids,)),
            dma((mids,)),
            dma((mids,)),
            dma((mids,)),
            dma((group,)),
            dma((group,)),
        ],
        compiler_params=pltpu.CompilerParams(
            collective_id=0, has_side_effects=True, vmem_limit_bytes=48 * 1024 * 1024),
    )(traces, centre_offset, foot_start, beam_count.reshape(1, -1), operator, high, low, weight)


def solution(mesh):
    return jax.shard_map(
        shards,
        mesh=mesh,
        in_specs=(
            P("off", ("grp", "mid"), "sub"),
            P(("grp", "mid")),
            P("grp", None),
            P("grp"),
            P("sub", "mid"),
        ),
        out_specs=P(("grp", "mid"), None),
        check_vma=False,
    )
```

time: 304 us -> 49.5 us (0.16)
  matrix products: 150 us -> 0 us
  waiting for transfers between devices: 67.9 us -> 0 us
  Pallas kernels: 0 us -> 42.4 us
  other arithmetic: 21.8 us -> 0 us
  local copies, waits for them, and re-layouts: 26.1 us -> 6.77 us
  between operations: 14.4 us -> 0.02 us
  starting transfers between devices: 12.5 us -> 0 us
  blocking collectives: 9.37 us -> 0 us
    dot_general x13 -> x0, matrix products: 150 us -> none  [the longest x8 36.7 us: add_block(): jnp.einsum('rsk,ksc->rsc', block_beams, kernels, preferred_element_type=j...]
    reduce_scatter x1 -> x0, waiting for transfers between devices: 55.4 us -> none  [shards(): lax.psum_scatter(partial_image, 'mid', scatter_dimension=0, tiled=True)]
    pallas_call x0 -> x1, Pallas kernels: none -> 42.4 us  [shards(): pl.pallas_call(functools.partial(kernel, (mids, offs, subs)), out_shape=j...]
    scatter-add x8 -> x0, other arithmetic: 16.6 us -> none  [add_block(): return partial_image.at[target].add(footprint.reshape(-1, DEPTH))]
    all_to_all x1 -> x0, waiting for transfers between devices: 11.5 us -> none  [shards(): lax.all_to_all(outgoing, 'mid', split_axis=1, concat_axis=0, tiled=True)]
    psum x1 -> x0, blocking collectives: 9.37 us -> none  [shards(): image_tile = lax.psum(tile_part, ('off', 'sub'))]
    all_to_all x1 -> x0, starting transfers between devices: 8.38 us -> none  [shards(): lax.all_to_all(outgoing, 'mid', split_axis=1, concat_axis=0, tiled=True)]
    gather x4 -> x0, local copies, waits for them, and re-layouts: 6.25 us -> none  [the longest x2 4.12 us: shards(): windows = padded[window_index]]
  transfers between devices with their start and end apart: 4 -> 0, of which waited for: 3 -> 0; matrix products, arithmetic and copies ran while one was open for 1% -> 0% of each run, Pallas kernels for 0% -> 0%
where the time goes in v1:
time: 49.5 us; the launch traced here: 49.2 us
  Pallas kernels  42.4 us (86%)
  local copies, waits for them, and re-layouts  6.77 us (14%)
    pallas_call x1, Pallas kernels, shards(): pl.pallas_call(functools.partial(kernel, (mids, offs, subs)), out_shape=j...  42.4 us
    unnamed x14, local copies, waits for them, and re-layouts  6.77 us

profile of v1, /device:TPU:0, one launch (start us, length us, event | category | flops | bytes accessed | tf_op | source)
XLA Modules:
  0.0 49.2 jit_solution(965461475348234188)
XLA Ops:
  0.0 0.8 %copy.9.start_ref = s32[256,16]{1,0:T(8,128)S(1)} copy(s32[256,16]{0,1:T(8,128)} %param.10) | data formatting | bytes 32768 | tf_op args[2]
  0.8 0.0 copy-start
  0.8 1.0 %copy-done = f32[2,17,8,512]{3,2,1,0:T(8,128)S(1)} copy-done((f32[2,17,8,512]{3,2,1,0:T(8,128)S(1)}, f32[2,17,8,512]{3,2,1,0:T(8,128)}, u32[]{:S(2)}) %copy-start) | copy-done | bytes 557080
  1.9 0.0 copy-start.1
  1.9 1.0 %copy-done.1 = bf16[256,1024]{1,0:T(8,128)(2,1)S(1)} copy-done((bf16[256,1024]{1,0:T(8,128)(2,1)S(1)}, bf16[256,1024]{1,0:T(8,128)(2,1)}, u32[]{:S(2)}) %copy-start.1) | copy-done | bytes 524312
  2.9 0.0 copy-start.2
  2.9 1.0 %copy-done.2 = bf16[256,1024]{1,0:T(8,128)(2,1)S(1)} copy-done((bf16[256,1024]{1,0:T(8,128)(2,1)S(1)}, bf16[256,1024]{1,0:T(8,128)(2,1)}, u32[]{:S(2)}) %copy-start.2) | copy-done | bytes 524312
  4.0 0.0 copy-start.3
  4.0 0.9 %copy-done.3 = bf16[1,64,1024]{2,1,0:T(8,128)(2,1)S(1)} copy-done((bf16[1,64,1024]{2,1,0:T(8,128)(2,1)S(1)}, bf16[1,64,1024]{2,1,0:T(8,128)(2,1)}, u32[]{:S(2)}) %copy-start.3) | copy-done | bytes 131096
  4.9 0.0 copy-start.4
  4.9 0.7 %copy-done.4 = s32[16]{0:T(128)S(1)} copy-done((s32[16]{0:T(128)S(1)}, s32[16]{0:T(128)}, u32[]{:S(2)}) %copy-start.4) | copy-done | bytes 88
  5.5 0.0 copy-start.5
  5.5 0.7 %copy-done.5 = s32[16]{0:T(128)S(1)} copy-done((s32[16]{0:T(128)S(1)}, s32[16]{0:T(128)}, u32[]{:S(2)}) %copy-start.5) | copy-done | bytes 88
  6.2 42.4 %shard_map.82 = f32[16,256]{1,0:T(8,128)S(1)} custom-call(bf16[64,1024]{1,0:T(8,128)(2,1)S(1)} %bitcast.2, s32[16]{0:T(128)S(1)} %copy-done.4, s32[256,16]{1,0:T(8,128)S(1)} %copy.9.start_ref, s32[1,16]{1,0:T(1,128)S(1)} %bitcast.3, bf16[1024,4096]{1,0:T(8,128)(2,1)} %operator_ref.1, bf16[256,1024]{1,0:T(8,128)(2,1)S(1)} %copy-done.2, ...), custom_call_target="tpu_custom_call" | custom-call | tf_op jit(solution)/shard_map/pallas_call | solution.py:278
  48.6 0.6 %copy.11 = f32[16,256]{1,0:T(8,128)} copy(f32[16,256]{1,0:T(8,128)S(1)} %shard_map.82) | data formatting | bytes 32768
Async XLA Ops:
  0.8 1.1 %copy-start = (f32[2,17,8,512]{3,2,1,0:T(8,128)S(1)}, f32[2,17,8,512]{3,2,1,0:T(8,128)}, u32[]{:S(2)}) copy-start(f32[2,17,8,512]{3,2,1,0:T(8,128)} %constant.8.clone.weight_ref) | copy-start | bytes 1671172
  1.9 1.0 %copy-start.1 = (bf16[256,1024]{1,0:T(8,128)(2,1)S(1)}, bf16[256,1024]{1,0:T(8,128)(2,1)}, u32[]{:S(2)}) copy-start(bf16[256,1024]{1,0:T(8,128)(2,1)} %constant.7.clone.low_ref) | copy-start | bytes 1572868
  2.9 1.0 %copy-start.2 = (bf16[256,1024]{1,0:T(8,128)(2,1)S(1)}, bf16[256,1024]{1,0:T(8,128)(2,1)}, u32[]{:S(2)}) copy-start(bf16[256,1024]{1,0:T(8,128)(2,1)} %constant.6.clone.high_ref) | copy-start | bytes 1572868
  4.0 0.9 %copy-start.3 = (bf16[1,64,1024]{2,1,0:T(8,128)(2,1)S(1)}, bf16[1,64,1024]{2,1,0:T(8,128)(2,1)}, u32[]{:S(2)}) copy-start(bf16[1,64,1024]{2,1,0:T(8,128)(2,1)} %param.8) | copy-start | bytes 393220
  4.9 0.7 %copy-start.4 = (s32[16]{0:T(128)S(1)}, s32[16]{0:T(128)}, u32[]{:S(2)}) copy-start(s32[16]{0:T(128)} %offset_ref.1) | copy-start | bytes 196
  5.5 0.7 %copy-start.5 = (s32[16]{0:T(128)S(1)}, s32[16]{0:T(128)}, u32[]{:S(2)}) copy-start(s32[16]{0:T(128)} %param.11) | copy-start | bytes 196

commit v2 on v1

v2 whole, which is shorter than its diff:
```python
import functools
import math

import jax
import jax.numpy as jnp
import numpy as np
from jax import lax
from jax.experimental import pallas as pl
from jax.experimental.pallas import tpu as pltpu
from jax.sharding import PartitionSpec as P

P_SIZE = 16
FL = 16
DEPTH = 256
HALF = 16
LANES = 128
F32 = jnp.float32
BF16 = jnp.bfloat16


def dft_quarter(total, parts):
    block = total // 2 // parts
    frequency = np.arange(total // 2)
    phase = 2.0 * np.pi / total * (np.arange(total // 4)[:, None] * frequency[None, :] % total)
    pair = np.stack([np.cos(phase), -np.sin(phase)]) / math.sqrt(total)
    pair = pair.reshape(2, total // 4, parts, block // LANES, LANES)
    table = pair.transpose(2, 1, 3, 0, 4).reshape(parts, total // 4, 2 * block).astype(np.float32)
    high = table.astype(BF16)
    low = (table - high.astype(np.float32)).astype(BF16)
    return high, low


def half_weights(total, parts):
    offsets = np.arange(-HALF, HALF + 1)
    taper = np.exp(-0.5 * (1.5 * offsets / HALF) ** 2)
    taper = (taper / np.sqrt(np.sum(taper * taper)))[HALF:]
    slopes = 0.25 * (np.arange(P_SIZE // 2, P_SIZE) - 0.5 * (P_SIZE - 1))
    theta = (
        2.0 * np.pi / total
        * np.arange(HALF + 1)[:, None, None] * slopes[None, :, None]
        * np.arange(total // 2)[None, None, :]
    )
    both = np.stack([np.cos(theta), np.sin(theta)]) * taper[None, :, None, None]
    both = both.reshape(2, HALF + 1, P_SIZE // 2, parts, -1).transpose(3, 0, 1, 2, 4)
    return both.astype(np.float32)


def kernel(
    sizes,
    traces_ref, offset_ref, start_ref, count_ref, operator_ref, high_ref, low_ref, weight_ref,
    out_ref,
    ext, high, low, weight, oper, spec, stage, send, recv, image, outgoing, parts, tile, peers,
    load_sem, oper_sem, halo_send, halo_recv, beam_send, beam_recv, part_send, part_recv,
    peer_send, peer_recv,
):
    mids, offs, subs = sizes
    rep = mids // P_SIZE
    me = lax.axis_index("mid")
    group = offs * subs
    mine = lax.axis_index("off") * subs + lax.axis_index("sub")
    rows = traces_ref.shape[0]
    total = traces_ref.shape[1]
    quarter = total // 4
    samples = operator_ref.shape[0]
    block = samples // 2
    chunks = block // LANES
    beams = offset_ref.shape[0]
    pairs = P_SIZE // 2
    laterals = operator_ref.shape[1] // DEPTH
    first_freq = lax.axis_index("sub") * block

    def member(k):
        other = lax.rem(mine + k, group)
        return other, {"off": other // subs, "sub": lax.rem(other, subs)}

    barrier = pltpu.get_barrier_semaphore()

    @pl.loop(1, mids)
    def _(k):
        pl.semaphore_signal(barrier, inc=1, device_id={"mid": lax.rem(me + k, mids)})

    @pl.loop(1, group)
    def _(k):
        pl.semaphore_signal(barrier, inc=1, device_id=member(k)[1])

    load_ext = pltpu.make_async_copy(traces_ref, ext.at[pl.ds(HALF, rows)], load_sem.at[0])
    load_high = pltpu.make_async_copy(high_ref, high, load_sem.at[1])
    load_low = pltpu.make_async_copy(low_ref, low, load_sem.at[2])
    load_weight = pltpu.make_async_copy(weight_ref, weight, load_sem.at[3])
    load_oper = [
        pltpu.make_async_copy(
            operator_ref.at[pl.ds(part * block + c * LANES, LANES)],
            oper.at[c, pl.ds(part * LANES, LANES)], oper_sem.at[c, part],
        )
        for c in range(chunks) for part in range(2)
    ]
    for load in (load_ext, load_high, load_low, load_weight, *load_oper):
        load.start()

    centres = start_ref.shape[1]
    slope = me // rep
    lateral_first = lax.rem(me, rep) * laterals
    at_slope = lax.broadcasted_iota(jnp.int32, start_ref.shape, 0) == slope
    starts = jnp.sum(jnp.where(at_slope, start_ref[...], 0), axis=0, keepdims=True)
    beam_id = lax.broadcasted_iota(jnp.int32, (1, centres), 1)
    counts = jnp.zeros((1, centres), jnp.int32)
    for t in range(mids):
        inside = (beam_id >= t * beams) & (beam_id < (t + 1) * beams)
        counts = jnp.where(inside, count_ref[t] + t * beams, counts)
    target = jnp.where(beam_id < counts, starts + lateral_first, -1)
    hot = (target == lax.broadcasted_iota(jnp.int32, (centres, centres), 0)).astype(F32)
    hot = hot.astype(BF16)

    pl.semaphore_wait(barrier, mids - 1 + group - 1)

    right, left = lax.rem(me + 1, mids), lax.rem(me + mids - 1, mids)
    to_right = pltpu.make_async_remote_copy(
        traces_ref.at[pl.ds(rows - HALF, HALF)], ext.at[pl.ds(0, HALF)],
        halo_send.at[0], halo_recv.at[0], device_id={"mid": right},
    )
    to_left = pltpu.make_async_remote_copy(
        traces_ref.at[pl.ds(0, HALF)], ext.at[pl.ds(HALF + rows, HALF)],
        halo_send.at[1], halo_recv.at[1], device_id={"mid": left},
    )
    to_right.start()
    to_left.start()

    def transform(c, pieces, keep, ranges):
        wide = slice(2 * c * LANES, 2 * (c + 1) * LANES)
        y = jnp.dot(pieces, high[:, wide], preferred_element_type=F32)
        y = y + jnp.dot(pieces, low[:, wide], preferred_element_type=F32)
        count = pieces.shape[0] // 4
        y0, y1, y2, y3 = (y[q * count:(q + 1) * count] for q in range(4))
        even_sum, even_dif, odd_sum, odd_dif = y0 + y2, y0 - y2, y1 + y3, y1 - y3
        f = first_freq + c * LANES + lax.broadcasted_iota(jnp.int32, (count, LANES), 1)
        sign = jnp.where(lax.rem(f, 4) < 2, 1.0, -1.0)
        odd = lax.rem(f, 2) == 1
        real = jnp.where(
            odd, even_dif[:, :LANES] + sign * odd_dif[:, LANES:],
            even_sum[:, :LANES] + sign * odd_sum[:, :LANES],
        ) * keep
        imag = jnp.where(
            odd, even_dif[:, LANES:] - sign * odd_dif[:, :LANES],
            even_sum[:, LANES:] + sign * odd_sum[:, LANES:],
        ) * keep
        for first, at, size in ranges:
            for part, value in enumerate((real, imag)):
                spec[c, part, at:at + size] = jnp.broadcast_to(
                    value[first:first + size, None, :], (size, pairs, LANES))

    load_ext.wait()
    load_high.wait()
    load_low.wait()
    own = jnp.concatenate(
        [ext[HALF:HALF + rows, q * quarter:(q + 1) * quarter] for q in range(4)], axis=0)
    for c in range(chunks):
        transform(c, own, 1.0, [(0, HALF, rows)])

    load_weight.wait()
    to_right.wait()
    to_left.wait()
    sides = [slice(0, HALF), slice(HALF + rows, 2 * HALF + rows)]
    edge = jnp.concatenate(
        [ext[side, q * quarter:(q + 1) * quarter] for q in range(4) for side in sides], axis=0)
    row = lax.broadcasted_iota(jnp.int32, (2 * HALF, LANES), 0)
    keep = jnp.where(row < HALF, (me > 0).astype(F32), (me < mids - 1).astype(F32))

    def beam_copy(c, k, to, source):
        return pltpu.make_async_remote_copy(
            send.at[c, to // rep],
            recv.at[c, pl.ds(pl.multiple_of(source * beams, beams), beams)],
            beam_send.at[c, k], beam_recv.at[c, source], device_id={"mid": to},
        )

    for c in range(chunks):
        transform(c, edge, keep, [(0, 0, HALF), (HALF, HALF + rows, HALF)])
        re = slice(c * LANES, (c + 1) * LANES)

        @pl.loop(0, beams)
        def _(b):
            centre = offset_ref[b] + HALF
            cos0 = weight[0, 0, :, re]
            a_re = cos0 * spec[c, 0, centre]
            a_im = cos0 * spec[c, 1, centre]
            b_re = jnp.zeros_like(a_re)
            b_im = jnp.zeros_like(a_re)
            for x in range(1, HALF + 1):
                r_up, r_dn = spec[c, 0, centre + x], spec[c, 0, centre - x]
                i_up, i_dn = spec[c, 1, centre + x], spec[c, 1, centre - x]
                cos, sin = weight[0, x, :, re], weight[1, x, :, re]
                a_re += cos * (r_up + r_dn)
                a_im += cos * (i_up + i_dn)
                b_re += sin * (i_up - i_dn)
                b_im += sin * (r_up - r_dn)
            at = pl.ds(pl.multiple_of(b * pairs, pairs), pairs)
            stage[c, 0, at, :] = a_re + b_re
            stage[c, 1, at, :] = a_im - b_im
            stage[c, 2, at, :] = a_re - b_re
            stage[c, 3, at, :] = a_im + b_im

        for p in range(pairs):
            for part in range(2):
                lanes = slice(part * LANES, (part + 1) * LANES)
                every = pl.ds(p, beams, stride=pairs)
                send[c, pairs + p, :, lanes] = stage.at[c, part][every, :].astype(BF16)
                send[c, pairs - 1 - p, :, lanes] = stage.at[c, 2 + part][every, :].astype(BF16)

        @pl.loop(0, mids - 1)
        def _(i):
            k = lax.rem(i + mids // 2, mids)
            k = jnp.where(i + mids // 2 >= mids, k + 1, k)
            beam_copy(c, k, lax.rem(me + k, mids), me).start()

        recv[c, pl.ds(pl.multiple_of(me * beams, beams), beams), :] = send[c, slope]

    for load in load_oper:
        load.wait()

    for c in range(chunks):
        @pl.loop(1, mids)
        def _(k):
            beam_copy(c, k, lax.rem(me + k, mids), lax.rem(me + mids - k, mids)).wait()

        gathered = jnp.dot(hot, recv[c], preferred_element_type=F32).astype(BF16)
        held = jnp.zeros((centres, DEPTH), F32)
        for l in reversed(range(laterals)):
            foot = jnp.dot(
                gathered, oper[c, :, l * DEPTH:(l + 1) * DEPTH], preferred_element_type=F32)
            held = foot if l == laterals - 1 else pltpu.roll(held, 1, 0) + foot
        image[...] = held if c == 0 else image[...] + held

    outgoing[...] = image[...].astype(BF16)

    def part_copy(k, to, source):
        return pltpu.make_async_remote_copy(
            outgoing.at[pl.ds(pl.multiple_of(to * beams, beams), beams)], parts.at[source],
            part_send.at[k], part_recv.at[source], device_id={"mid": to},
        )

    @pl.loop(1, mids)
    def _(k):
        part_copy(k, lax.rem(me + k, mids), me).start()

    home = pl.ds(pl.multiple_of(me * beams, beams), beams)
    parts[me] = outgoing[home, :]

    @pl.loop(1, mids)
    def _(k):
        part_copy(k, lax.rem(me + k, mids), lax.rem(me + mids - k, mids)).wait()

    tile[...] = jnp.sum(parts[...].astype(F32), axis=0) * (1.0 / math.sqrt(FL * P_SIZE))

    def peer_copy(k, to, source):
        return pltpu.make_async_remote_copy(
            tile, peers.at[source], peer_send.at[k], peer_recv.at[source], device_id=to,
        )

    @pl.loop(1, group)
    def _(k):
        peer_copy(k, member(k)[1], mine).start()

    peers[mine] = tile[...]

    @pl.loop(1, group)
    def _(k):
        peer_copy(k, member(k)[1], lax.rem(mine + group - k, group)).wait()

    out_ref[...] = jnp.sum(peers[...], axis=0)


def shards(traces, centre_offset, foot_start, beam_count, operator):
    mids, offs, subs = (lax.axis_size(name) for name in ("mid", "off", "sub"))
    traces = traces[0]
    if subs > 1:
        traces = lax.all_gather(traces, "sub", axis=1, tiled=True)
    rows, total = traces.shape
    samples, columns = operator.shape
    beams = centre_offset.shape[0]
    centres = foot_start.shape[0]
    group = offs * subs
    high, low = dft_quarter(total, subs)
    weight = half_weights(total, subs)
    pick = (lambda table: table[0]) if subs == 1 else (
        lambda table: lax.dynamic_index_in_dim(jnp.asarray(table), lax.axis_index("sub"), 0, False))
    high, low, weight = (jnp.asarray(pick(table)) for table in (high, low, weight))
    vmem = pl.BlockSpec(memory_space=pltpu.VMEM)
    smem = pl.BlockSpec(memory_space=pltpu.SMEM)
    hbm = pl.BlockSpec(memory_space=pl.ANY)
    dma = pltpu.SemaphoreType.DMA
    chunks = samples // 2 // LANES
    return pl.pallas_call(
        functools.partial(kernel, (mids, offs, subs)),
        out_shape=jax.ShapeDtypeStruct((beams, DEPTH), F32),
        in_specs=[hbm, smem, vmem, smem, hbm, hbm, hbm, hbm],
        out_specs=vmem,
        scratch_shapes=[
            pltpu.VMEM((rows + 2 * HALF, total), BF16),
            pltpu.VMEM(high.shape, BF16),
            pltpu.VMEM(low.shape, BF16),
            pltpu.VMEM(weight.shape, F32),
            pltpu.VMEM((chunks, 2 * LANES, columns), BF16),
            pltpu.VMEM((chunks, 2, rows + 2 * HALF, P_SIZE // 2, LANES), F32),
            pltpu.VMEM((chunks, 4, beams * P_SIZE // 2, LANES), F32),
            pltpu.VMEM((chunks, P_SIZE, beams, 2 * LANES), BF16),
            pltpu.VMEM((chunks, mids * beams, 2 * LANES), BF16),
            pltpu.VMEM((centres, DEPTH), F32),
            pltpu.VMEM((centres, DEPTH), BF16),
            pltpu.VMEM((mids, beams, DEPTH), BF16),
            pltpu.VMEM((beams, DEPTH), F32),
            pltpu.VMEM((group, beams, DEPTH), F32),
            dma((4,)),
            dma((chunks, 2)),
            dma((2,)),
            dma((2,)),
            dma((chunks, mids)),
            dma((chunks, mids)),
            dma((mids,)),
            dma((mids,)),
            dma((group,)),
            dma((group,)),
        ],
        compiler_params=pltpu.CompilerParams(
            collective_id=0, has_side_effects=True, vmem_limit_bytes=67043328),
    )(traces, centre_offset, foot_start.T, beam_count, operator, high, low, weight)


def solution(mesh):
    return jax.shard_map(
        shards,
        mesh=mesh,
        in_specs=(
            P("off", ("grp", "mid"), "sub"),
            P(("grp", "mid")),
            P("grp", None),
            P("grp"),
            P("sub", "mid"),
        ),
        out_specs=P(("grp", "mid"), None),
        check_vma=False,
    )
```

time: 49.5 us -> 36.8 us (0.74)
  Pallas kernels: 42.4 us -> 35.1 us
  local copies, waits for them, and re-layouts: 6.77 us -> 1.32 us
    pallas_call x1, Pallas kernels: 42.4 us -> 35.1 us  [shards(): pl.pallas_call(functools.partial(kernel, (mids, offs, subs)), out_shape=j...]
    unnamed x14 -> x1, local copies, waits for them, and re-layouts: 6.77 us -> 1.32 us
where the time goes in v2:
time: 36.8 us; the launch traced here: 36.5 us
  Pallas kernels  35.1 us (95%)
  local copies, waits for them, and re-layouts  1.32 us (4%)
    pallas_call x1, Pallas kernels, shards(): pl.pallas_call(functools.partial(kernel, (mids, offs, subs)), out_shape=j...  35.1 us
    unnamed x1, local copies, waits for them, and re-layouts  1.32 us

profile of v2, /device:TPU:0, one launch (start us, length us, event | category | flops | bytes accessed | tf_op | source)
XLA Modules:
  0.0 36.5 jit_solution(11223983176033130620)
XLA Ops:
  0.0 35.1 %shard_map.82 = f32[16,256]{1,0:T(8,128)} custom-call(bf16[64,1024]{1,0:T(8,128)(2,1)} %bitcast.2, s32[16]{0:T(128)} %offset_ref.1, s32[16,256]{1,0:T(8,128)} %bitcast.3, s32[16]{0:T(128)} %count_ref.1, bf16[1024,4096]{1,0:T(8,128)(2,1)} %operator_ref.1, bf16[256,1024]{1,0:T(8,128)(2,1)} %constant.6.clone.high_ref, bf16[256,1024]{1,0:T(8,128)(2,1)} %constant.7.clone.low_ref, ...), custom_call_target="tpu_custom_call" | custom-call | tf_op jit(solution)/shard_map/pallas_call | solution.py:291
  35.2 1.3 %copy.10 = f32[16,256]{1,0:T(8,128)} copy(f32[16,256]{1,0:T(8,128)} %shard_map.82) | data formatting | bytes 32768

commit v3 on v2

--- a/solution.py
+++ b/solution.py
@@ -48,8 +48,8 @@
 def kernel(
     sizes,
     traces_ref, offset_ref, start_ref, count_ref, operator_ref, high_ref, low_ref, weight_ref,
-    out_ref,
-    ext, high, low, weight, oper, spec, stage, send, recv, image, outgoing, parts, tile, peers,
+    peers,
+    ext, high, low, weight, oper, spec, stage, send, recv, image, outgoing, parts, tile,
     load_sem, oper_sem, halo_send, halo_recv, beam_send, beam_recv, part_send, part_recv,
     peer_send, peer_recv,
 ):
@@ -67,6 +67,8 @@
     beams = offset_ref.shape[0]
     pairs = P_SIZE // 2
     laterals = operator_ref.shape[1] // DEPTH
+    centres = start_ref.shape[1]
+    slope = me // rep
     first_freq = lax.axis_index("sub") * block
 
     def member(k):
@@ -96,20 +98,6 @@
     ]
     for load in (load_ext, load_high, load_low, load_weight, *load_oper):
         load.start()
-
-    centres = start_ref.shape[1]
-    slope = me // rep
-    lateral_first = lax.rem(me, rep) * laterals
-    at_slope = lax.broadcasted_iota(jnp.int32, start_ref.shape, 0) == slope
-    starts = jnp.sum(jnp.where(at_slope, start_ref[...], 0), axis=0, keepdims=True)
-    beam_id = lax.broadcasted_iota(jnp.int32, (1, centres), 1)
-    counts = jnp.zeros((1, centres), jnp.int32)
-    for t in range(mids):
-        inside = (beam_id >= t * beams) & (beam_id < (t + 1) * beams)
-        counts = jnp.where(inside, count_ref[t] + t * beams, counts)
-    target = jnp.where(beam_id < counts, starts + lateral_first, -1)
-    hot = (target == lax.broadcasted_iota(jnp.int32, (centres, centres), 0)).astype(F32)
-    hot = hot.astype(BF16)
 
     pl.semaphore_wait(barrier, mids - 1 + group - 1)
 
@@ -153,8 +141,7 @@
     load_low.wait()
     own = jnp.concatenate(
         [ext[HALF:HALF + rows, q * quarter:(q + 1) * quarter] for q in range(4)], axis=0)
-    for c in range(chunks):
-        transform(c, own, 1.0, [(0, HALF, rows)])
+    transform(0, own, 1.0, [(0, HALF, rows)])
 
     load_weight.wait()
     to_right.wait()
@@ -173,6 +160,8 @@
         )
 
     for c in range(chunks):
+        if c > 0:
+            transform(c, own, 1.0, [(0, HALF, rows)])
         transform(c, edge, keep, [(0, 0, HALF), (HALF, HALF + rows, HALF)])
         re = slice(c * LANES, (c + 1) * LANES)
 
@@ -213,6 +202,18 @@
 
         recv[c, pl.ds(pl.multiple_of(me * beams, beams), beams), :] = send[c, slope]
 
+    lateral_first = lax.rem(me, rep) * laterals
+    at_slope = lax.broadcasted_iota(jnp.int32, start_ref.shape, 0) == slope
+    starts = jnp.sum(jnp.where(at_slope, start_ref[...], 0), axis=0, keepdims=True)
+    beam_id = lax.broadcasted_iota(jnp.int32, (1, centres), 1)
+    counts = jnp.zeros((1, centres), jnp.int32)
+    for t in range(mids):
+        inside = (beam_id >= t * beams) & (beam_id < (t + 1) * beams)
+        counts = jnp.where(inside, count_ref[t] + t * beams, counts)
+    target = jnp.where(beam_id < counts, starts + lateral_first, -1)
+    hot = (target == lax.broadcasted_iota(jnp.int32, (centres, centres), 0)).astype(F32)
+    hot = hot.astype(BF16)
+
     for load in load_oper:
         load.wait()
 
@@ -264,8 +265,6 @@
     @pl.loop(1, group)
     def _(k):
         peer_copy(k, member(k)[1], lax.rem(mine + group - k, group)).wait()
-
-    out_ref[...] = jnp.sum(peers[...], axis=0)
 
 
 def shards(traces, centre_offset, foot_start, beam_count, operator):
@@ -285,12 +284,12 @@
     high, low, weight = (jnp.asarray(pick(table)) for table in (high, low, weight))
     vmem = pl.BlockSpec(memory_space=pltpu.VMEM)
     smem = pl.BlockSpec(memory_space=pltpu.SMEM)
-    hbm = pl.BlockSpec(memory_space=pl.ANY)
+    hbm = pl.BlockSpec(memory_space=pltpu.HBM)
     dma = pltpu.SemaphoreType.DMA
     chunks = samples // 2 // LANES
-    return pl.pallas_call(
+    shares = pl.pallas_call(
         functools.partial(kernel, (mids, offs, subs)),
-        out_shape=jax.ShapeDtypeStruct((beams, DEPTH), F32),
+        out_shape=jax.ShapeDtypeStruct((group, beams, DEPTH), F32),
         in_specs=[hbm, smem, vmem, smem, hbm, hbm, hbm, hbm],
         out_specs=vmem,
         scratch_shapes=[
@@ -307,7 +306,6 @@
             pltpu.VMEM((centres, DEPTH), BF16),
             pltpu.VMEM((mids, beams, DEPTH), BF16),
             pltpu.VMEM((beams, DEPTH), F32),
-            pltpu.VMEM((group, beams, DEPTH), F32),
             dma((4,)),
             dma((chunks, 2)),
             dma((2,)),
@@ -322,6 +320,7 @@
         compiler_params=pltpu.CompilerParams(
             collective_id=0, has_side_effects=True, vmem_limit_bytes=67043328),
     )(traces, centre_offset, foot_start.T, beam_count, operator, high, low, weight)
+    return jnp.sum(shares, axis=0)
 
 
 def solution(mesh):

time: 36.8 us -> 36.7 us (level)
  other arithmetic: 0 us -> 1.37 us
  local copies, waits for them, and re-layouts: 1.32 us -> 0 us
    reduce_sum x0 -> x1, other arithmetic: none -> 1.37 us  [shards(): return jnp.sum(shares, axis=0)]
    unnamed x1 -> x0, local copies, waits for them, and re-layouts: 1.32 us -> none
where the time goes in v3:
time: 36.7 us; the launch traced here: 36.5 us
  Pallas kernels  35.1 us (96%)
  other arithmetic  1.37 us (4%)
    pallas_call x1, Pallas kernels, shards(): pl.pallas_call(functools.partial(kernel, (mids, offs, subs)), out_shape=j...  35.1 us
    reduce_sum x1, other arithmetic, shards(): return jnp.sum(shares, axis=0)  1.37 us

profile of v3, /device:TPU:0, one launch (start us, length us, event | category | flops | bytes accessed | tf_op | source)
XLA Modules:
  0.0 36.5 jit_solution(13480192037624672914)
XLA Ops:
  0.0 35.1 %shard_map.82 = f32[2,16,256]{2,1,0:T(8,128)} custom-call(bf16[64,1024]{1,0:T(8,128)(2,1)} %bitcast.2, s32[16]{0:T(128)} %offset_ref.1, s32[16,256]{1,0:T(8,128)} %bitcast.3, s32[16]{0:T(128)} %count_ref.1, bf16[1024,4096]{1,0:T(8,128)(2,1)} %operator_ref.1, bf16[256,1024]{1,0:T(8,128)(2,1)} %constant.8.clone.high_ref, ...), custom_call_target="tpu_custom_call" | custom-call | tf_op jit(solution)/shard_map/pallas_call | solution.py:290
  35.1 1.4 %reduce_sum.9 = f32[16,256]{1,0:T(8,128)} reduce(f32[2,16,256]{2,1,0:T(8,128)} %shard_map.82, f32[]{:T(128)} %constant.3.clone.1), dimensions={0}, to_apply=%region_0.0 | reduce | flops 4096 | bytes 49156 | tf_op jit(solution)/shard_map/reduce_sum | solution.py:323
